TPU v7x, 32 devices: a whole 2x2x4 slice. The times are simulated.
32 devices in a mesh: seq: 8 (over y, x, core), wt: 4 (over z).
Axes of the slice: x: 2, y: 2, z: 4, core: 2. Of those that a mesh axis runs over, the one named last changes fastest.
Arguments:
- layer_input: bfloat16 [1024, 2048], P(('seq', 'wt')), may hold values from -6 to 6
- token_shift_rates: float32 [5, 2048], replicated, may hold values from 0 to 1
- input_projection_weight: bfloat16 [3, 2048, 2048], P(None, None, 'wt'), may hold values from -0.125 to 0.125
- output_matrix: bfloat16 [2048, 2048], P('wt'), may hold values from -0.125 to 0.125
- decay_lowrank_first: bfloat16 [2048, 96], replicated, may hold values from -0.125 to 0.125
- decay_lowrank_second: bfloat16 [96, 2048], P(None, 'wt'), may hold values from -0.625 to 0.625
- learning_rate_first: bfloat16 [2048, 96], replicated, may hold values from -0.125 to 0.125
- learning_rate_second: bfloat16 [96, 2048], P(None, 'wt'), may hold values from -0.625 to 0.625
- decay_channel_bias: float32 [2048], P('wt'), may hold values from -10 to 1
- learning_rate_bias: float32 [2048], P('wt'), may hold values from -6 to 2
- prenorm_key_scale: float32 [2048], P('wt'), may hold values from 0.5 to 1.5
- written_key_share: float32 [2048], P('wt'), may hold values from 0 to 1
- present_step_coefficient: float32 [2048], P('wt'), may hold values from -3 to 3
- head_norm_gain: float32 [2048], P('wt'), may hold values from 0.5 to 1.5
- packed_request_length: int32 [8], replicated, may hold values from 1 to 512, 1024 in all
Outputs:
- layer_out: bfloat16 [1024, 2048], P(('seq', 'wt'))
Inputs may be any that keep to these rules, and one draw needn't show every extreme that they name: `packed_request_length`: the 8 lengths sum to 1024, and the longest is exactly 512.
All inputs are finite; a program needn't handle non-finite values.
Results may differ from a plain program's by a relative error of at most 0.0069.
Values may be sent and summed in bfloat16 or wider, within the bound.
A program may use at most 128 MiB of HBM per device.

v0:
```python
import functools
import jax
import jax.numpy as jnp
from jax import lax
from jax.experimental import pallas as pl
from jax.experimental.pallas import tpu as pltpu
from jax.sharding import PartitionSpec as P

HS = 64
LOG_SCALE = 0.6065306597126334
MESH = pl.DeviceIdType.MESH
F32 = jnp.float32
BF16 = jnp.bfloat16
STATE_TYPE = BF16


def mm(a, b, ca=1, cb=0):
    return lax.dot_general(
        a.astype(BF16), b.astype(BF16), (((ca,), (cb,)), ((), ())), preferred_element_type=F32
    )


def mm_full(a, b, ca=1, cb=0):
    return lax.dot_general(
        a, b, (((ca,), (cb,)), ((), ())), preferred_element_type=F32, precision=lax.Precision.HIGHEST
    )


def token_tables(first, rows, lengths):
    pos_c = first + lax.broadcasted_iota(jnp.int32, (rows, 1), 0)
    pos_r = first + lax.broadcasted_iota(jnp.int32, (1, rows), 1)
    far = jnp.int32(2**30)
    start = jnp.int32(0)
    reset = jnp.zeros((rows, 1), jnp.int32)
    seg_c = jnp.zeros((rows, 1), jnp.int32)
    seg_r = jnp.zeros((1, rows), jnp.int32)
    seg_last = jnp.int32(0)
    for length in lengths:
        reset = jnp.maximum(reset, jnp.where(pos_c == start, 1, 0))
        inside = jnp.where(start >= first, start, far)
        seg_c = seg_c + jnp.where(pos_c >= inside, 1, 0)
        seg_r = seg_r + jnp.where(pos_r >= inside, 1, 0)
        seg_last = seg_last + jnp.where(first + (rows - 1) >= inside, 1, 0)
        start = start + length
    return reset, seg_c, seg_r, seg_last


def head_slice(h):
    return slice(h * HS, (h + 1) * HS)


def per_head(fn, width):
    return jnp.concatenate([fn(head_slice(h)) for h in range(width // HS)], axis=1)


def block_terms(recept, keys, values, decay_in, rate_in, chan, seg_c, seg_r, seg_last):
    rows, width = keys.shape
    heads = width // HS
    decay_bias, rate_bias, key_scale, share = (chan[i : i + 1] for i in range(4))
    logw = -LOG_SCALE * jax.nn.sigmoid(decay_bias + decay_in)
    rate = jax.nn.sigmoid(rate_bias + rate_in)
    row = lax.broadcasted_iota(jnp.int32, (rows, rows), 0)
    col = lax.broadcasted_iota(jnp.int32, (rows, rows), 1)
    tri = jnp.where(row >= col, 1.0, 0.0).astype(F32)
    cum = mm_full(tri, logw)
    center = cum[rows // 2 - 1 : rows // 2]
    last = cum[rows - 1 : rows]
    grow = jnp.exp(cum - center)
    grow_x = jnp.exp(cum - logw - center)
    shrink = jnp.exp(center - cum)
    to_start = jnp.exp(center) * jnp.where(seg_c == 0, 1.0, 0.0)
    to_end = jnp.exp(last - center) * jnp.where(seg_c == seg_last, 1.0, 0.0)
    scaled = keys * key_scale
    squares = scaled * scaled
    norm = per_head(
        lambda s: jnp.broadcast_to(
            lax.rsqrt(jnp.sum(squares[:, s], axis=1, keepdims=True) + 1e-06), (rows, HS)
        ),
        width,
    )
    unit = scaled * norm
    keys_mod = keys * (1.0 + (rate - 1.0) * share)
    u_c = unit * grow_x
    q_c = recept * grow
    r_c = unit * rate * shrink
    k_c = keys_mod * shrink
    u_0 = u_c * to_start
    q_0 = q_c * to_start
    r_e = r_c * to_end
    k_e = k_c * to_end
    same = seg_c == seg_r
    strict = jnp.logical_and(same, row > col)
    causal = jnp.logical_and(same, row >= col)
    a_ur, a_uk, a_qr, a_qk = [], [], [], []
    for h in range(heads):
        s = head_slice(h)
        left = jnp.concatenate([u_c[:, s], q_c[:, s]], axis=0)
        right = jnp.concatenate([r_c[:, s], k_c[:, s]], axis=0)
        pair = mm(left, right, 1, 1)
        a_ur.append(jnp.where(strict, pair[:rows, :rows], 0.0))
        a_uk.append(jnp.where(strict, pair[:rows, rows:], 0.0).astype(BF16))
        a_qr.append(jnp.where(causal, pair[rows:, :rows], 0.0).astype(BF16))
        a_qk.append(jnp.where(causal, pair[rows:, rows:], 0.0).astype(BF16))
    eye = jnp.where(row == col, 1.0, 0.0)
    inverse = None
    size = 1
    while size < rows:
        tile_r, tile_c = row // size, col // size
        corner = jnp.logical_and(tile_r == tile_c + 1, tile_r % 2 == 1)
        lows = [jnp.where(corner, a, 0.0) for a in a_ur]
        if inverse is None:
            inverse = [eye - low for low in lows]
        else:
            halves = [mm(x, low) for x, low in zip(inverse, lows)]
            inverse = [x - mm(half, x) for x, half in zip(inverse, halves)]
        size *= 2
    small_r = lax.broadcasted_iota(jnp.int32, (HS, HS), 0)
    small_c = lax.broadcasted_iota(jnp.int32, (HS, HS), 1)
    decay_all = jnp.exp(last) * jnp.where(seg_last == 0, 1.0, 0.0)
    reads, offsets, maps, adds = [], [], [], []
    for h in range(heads):
        s = head_slice(h)
        v = values[:, s].astype(BF16)
        kv = mm(jnp.concatenate([a_uk[h], a_qk[h]], axis=0), v)
        solved = mm(inverse[h], jnp.concatenate([u_0[:, s], kv[:rows]], axis=1))
        out = jnp.concatenate([q_0[:, s], kv[rows:]], axis=1) - mm(a_qr[h], solved)
        reads.append(out[:, :HS])
        offsets.append(out[:, HS:])
        end = mm(r_e[:, s], solved, 0, 0)
        diag = jnp.where(small_r == small_c, jnp.broadcast_to(decay_all[:, s], (HS, HS)), 0.0)
        maps.append(diag - end[:, :HS])
        adds.append(mm(k_e[:, s], v, 0, 0) - end[:, HS:])
    return reads, offsets, maps, adds, keys_mod


def finish_heads(heads_y, recept, keys_mod, values, coefficient, gain):
    own = recept * keys_mod * coefficient
    mixed = []
    for h, y in enumerate(heads_y):
        s = head_slice(h)
        centered = y - jnp.mean(y, axis=1, keepdims=True)
        spread = jnp.mean(centered * centered, axis=1, keepdims=True)
        normed = centered * lax.rsqrt(spread + 0.00064) * gain[:, s]
        mixed.append(normed + jnp.sum(own[:, s], axis=1, keepdims=True) * values[:, s])
    return jnp.concatenate(mixed, axis=1).astype(BF16)


def kernel(
    n_seq, n_wt, hops,
    x_ref, rates_ref, win_hbm, wout_hbm, d1_ref, d2_ref, a1_ref, a2_ref, chan_ref, len_ref,
    out_ref,
    x_all, edge_src, edge_in, win, wout, lo_src, lo_in, part, part_16, rs_in,
    w_sem, edge_sem, fwd_sem, x_send, x_recv, lo_send, lo_recv, rs_send, rs_recv,
):
    b = lax.axis_index("seq")
    w = lax.axis_index("wt")
    shard, model = x_ref.shape
    rows = shard * n_wt
    width = win.shape[2]
    heads = width // HS
    piece = model // 8

    loads = [pltpu.make_async_copy(win_hbm.at[c], win.at[c], w_sem.at[c]) for c in range(3)]
    loads.append(pltpu.make_async_copy(wout_hbm, wout, w_sem.at[3]))
    for load in loads:
        load.start()

    def wt_peer(d):
        return (b, lax.rem(w + d, n_wt))

    def seq_peer(d):
        return (lax.rem(b + d, n_seq), w)

    barrier = pltpu.get_barrier_semaphore()
    for d in range(1, n_wt):
        pl.semaphore_signal(barrier, inc=1, device_id=wt_peer(d), device_id_type=MESH)
    for d in range(1, n_seq):
        pl.semaphore_signal(barrier, inc=1, device_id=seq_peer(d), device_id_type=MESH)
    last_row = x_ref[shard - 1 : shard, :].astype(F32)
    for i in range(8):
        edge_src[i : i + 1, :] = last_row[:, i * piece : (i + 1) * piece]
    mine = pl.ds(pl.multiple_of(w * shard, shard), shard)
    x_all[mine, :] = x_ref[...]
    pl.semaphore_wait(barrier, n_wt + n_seq - 2)

    def remote(src, dst, send, recv, target):
        return pltpu.make_async_remote_copy(
            src_ref=src, dst_ref=dst, send_sem=send, recv_sem=recv, device_id=target, device_id_type=MESH
        )

    edge_copy = remote(edge_src, edge_in, edge_sem.at[0], edge_sem.at[1], seq_peer(1))
    forwards = [
        remote(edge_in, edge_in, fwd_sem.at[d - 1], edge_sem.at[1], wt_peer(d)) for d in range(1, n_wt)
    ]
    is_last = w == n_wt - 1

    @pl.when(is_last)
    def _():
        edge_copy.start()

    x_copies = [
        remote(x_ref, x_all.at[mine], x_send.at[d - 1], x_recv.at[d - 1], wt_peer(d))
        for d in range(1, n_wt)
    ]
    for copy in x_copies:
        copy.start()
    edge_copy.wait_recv()

    @pl.when(is_last)
    def _():
        for copy in forwards:
            copy.start()
        edge_copy.wait_send()
        for copy in forwards:
            copy.wait_send()

    for copy in x_copies:
        copy.wait_recv()
    for load in loads[:3]:
        load.wait()

    lengths = [len_ref[i] for i in range(len_ref.shape[0])]
    reset, seg_c, seg_r, seg_last = token_tables(b * rows, rows, lengths)
    edge = jnp.concatenate([edge_in[i : i + 1, :] for i in range(8)], axis=1)
    first_row = lax.broadcasted_iota(jnp.int32, (rows, 1), 0) == 0
    sums = [None] * 5
    step = min(512, model)
    for k in range(0, model, step):
        cols = slice(k, k + step)
        current = x_all[:, cols].astype(F32)
        previous = jnp.where(first_row, edge[:, cols], pltpu.roll(current, 1, 0))
        previous = jnp.where(reset == 1, 0.0, previous)
        delta = previous - current
        for c in range(5):
            mixed = (current + delta * rates_ref[c : c + 1, cols]).astype(BF16)
            weight = (
                win[c, cols, :] if c < 3 else (d1_ref if c == 3 else a1_ref)[cols, :]
            )
            term = jnp.dot(mixed, weight, preferred_element_type=F32)
            sums[c] = term if sums[c] is None else sums[c] + term
    recept, keys, values = sums[:3]
    decay_in = jnp.dot(jnp.tanh(sums[3]).astype(BF16), d2_ref[...], preferred_element_type=F32)
    rate_in = jnp.dot(sums[4].astype(BF16), a2_ref[...], preferred_element_type=F32)
    chan = chan_ref[...]
    reads, offsets, maps, adds, keys_mod = block_terms(
        recept, keys, values, decay_in, rate_in, chan, seg_c, seg_r, seg_last
    )
    for h in range(heads):
        lo_src[0, :, head_slice(h)] = maps[h].astype(STATE_TYPE)
        lo_src[1, :, head_slice(h)] = adds[h].astype(STATE_TYPE)
    lo_copies = [
        remote(lo_src, lo_in.at[d - 1], lo_send.at[d - 1], lo_recv.at[d - 1], seq_peer(d))
        for d in range(1, hops)
    ]
    lo_copies.append(
        remote(
            lo_src.at[1], lo_in.at[hops - 1, 1], lo_send.at[hops - 1], lo_recv.at[hops - 1], seq_peer(hops)
        )
    )
    for copy in lo_copies:
        copy.start()
    for copy in lo_copies:
        copy.wait_recv()
    state = [lo_in[hops - 1, 1, :, head_slice(h)].astype(F32) for h in range(heads)]
    for d in range(hops - 2, -1, -1):
        state = [
            mm(lo_in[d, 0, :, head_slice(h)], state[h]) + lo_in[d, 1, :, head_slice(h)].astype(F32)
            for h in range(heads)
        ]
    heads_y = [mm(reads[h], state[h]) + offsets[h] for h in range(heads)]
    head_mix = finish_heads(heads_y, recept, keys_mod, values, chan[4:5], chan[5:6])

    loads[3].wait()
    for k in range(0, model, step):
        cols = slice(k, k + step)
        term = jnp.dot(head_mix, wout[:, cols], preferred_element_type=F32)
        part[:, cols] = term
        part_16[:, cols] = term.astype(BF16)
    rs_copies = []
    for d in range(1, n_wt):
        there = pl.ds(pl.multiple_of(lax.rem(w + d, n_wt) * shard, shard), shard)
        rs_copies.append(
            remote(part_16.at[there], rs_in.at[d - 1], rs_send.at[d - 1], rs_recv.at[d - 1], wt_peer(d))
        )
    for copy in rs_copies:
        copy.start()
    total = part[mine, :] + x_ref[...].astype(F32)
    for d, copy in enumerate(rs_copies):
        copy.wait_recv()
        total = total + rs_in[d].astype(F32)
    out_ref[...] = total.astype(out_ref.dtype)
    for copy in x_copies + lo_copies + rs_copies:
        copy.wait_send()


def shards(
    n_seq, n_wt,
    layer_input, token_shift_rates, input_projection_weight, output_matrix,
    decay_lowrank_first, decay_lowrank_second, learning_rate_first, learning_rate_second,
    decay_channel_bias, learning_rate_bias, prenorm_key_scale, written_key_share,
    present_step_coefficient, head_norm_gain, packed_request_length,
):
    shard, model = layer_input.shape
    rows = shard * n_wt
    width = decay_lowrank_second.shape[1]
    hops = (n_seq + 1) // 2
    chan = jnp.stack(
        [
            decay_channel_bias, learning_rate_bias, prenorm_key_scale,
            written_key_share, present_step_coefficient, head_norm_gain,
        ]
    )
    vmem = pl.BlockSpec(memory_space=pltpu.VMEM)
    far = pl.BlockSpec(memory_space=pl.ANY)
    dma = pltpu.SemaphoreType.DMA
    return pl.pallas_call(
        functools.partial(kernel, n_seq, n_wt, hops),
        out_shape=jax.ShapeDtypeStruct((shard, model), BF16),
        in_specs=[vmem, vmem, far, far, vmem, vmem, vmem, vmem, vmem, pl.BlockSpec(memory_space=pltpu.SMEM)],
        out_specs=vmem,
        scratch_shapes=[
            pltpu.VMEM((rows, model), BF16),
            pltpu.VMEM((8, model // 8), F32),
            pltpu.VMEM((8, model // 8), F32),
            pltpu.VMEM((3, model, width), BF16),
            pltpu.VMEM((width, model), BF16),
            pltpu.VMEM((2, HS, width), STATE_TYPE),
            pltpu.VMEM((hops, 2, HS, width), STATE_TYPE),
            pltpu.VMEM((rows, model), F32),
            pltpu.VMEM((rows, model), BF16),
            pltpu.VMEM((n_wt - 1, shard, model), BF16),
            dma((4,)), dma((2,)), dma((n_wt - 1,)),
            dma((n_wt - 1,)), dma((n_wt - 1,)),
            dma((hops,)), dma((hops,)),
            dma((n_wt - 1,)), dma((n_wt - 1,)),
        ],
        compiler_params=pltpu.CompilerParams(
            collective_id=0, has_side_effects=True, vmem_limit_bytes=56 * 1024 * 1024
        ),
    )(
        layer_input, token_shift_rates, input_projection_weight, output_matrix,
        decay_lowrank_first, decay_lowrank_second, learning_rate_first, learning_rate_second,
        chan, packed_request_length,
    )


def solution(mesh):
    placed = (
        P(("seq", "wt"), None),
        P(),
        P(None, None, "wt"),
        P("wt", None),
        P(),
        P(None, "wt"),
        P(),
        P(None, "wt"),
        P("wt"),
        P("wt"),
        P("wt"),
        P("wt"),
        P("wt"),
        P("wt"),
        P(),
    )
    return jax.shard_map(
        functools.partial(shards, mesh.shape["seq"], mesh.shape["wt"]),
        mesh=mesh, in_specs=placed, out_specs=P(("seq", "wt"), None), check_vma=False,
    )
```

profile of v0, /device:TPU:24, one launch (start us, length us, event | category | flops | bytes accessed | tf_op | source)
XLA Modules:
  0.0 57.1 jit_solution(6987325449687789171)
XLA Ops:
  0.0 1.4 %stack.27.chan_ref = f32[6,512]{1,0:T(8,128)} concatenate(f32[1,512]{1,0:T(1,128)} %bitcast.6, f32[1,512]{1,0:T(1,128)} %bitcast.7, f32[1,512]{1,0:T(1,128)} %bitcast.8, f32[1,512]{1,0:T(1,128)} %bitcast.9, f32[1,512]{1,0:T(1,128)} %bitcast.10, f32[1,512]{1,0:T(1,128)} %bitcast.11), dimensions={0} | concatenate | bytes 24576 | tf_op jit(solution)/shard_map/stack | solution.py:307
  1.4 2.0 %copy.16.d1_ref = bf16[2048,96]{1,0:T(8,128)(2,1)} copy(bf16[2048,96]{0,1:T(8,128)(2,1)} %param.19) | data formatting | bytes 786432 | tf_op args[4]
  3.4 2.0 %copy.17.a1_ref = bf16[2048,96]{1,0:T(8,128)(2,1)} copy(bf16[2048,96]{0,1:T(8,128)(2,1)} %param.21) | data formatting | bytes 786432 | tf_op args[6]
  5.4 50.1 %shard_map.145 = bf16[32,2048]{1,0:T(8,128)(2,1)} custom-call(bf16[32,2048]{1,0:T(8,128)(2,1)} %x_ref.1, f32[5,2048]{1,0:T(8,128)} %rates_ref.1, bf16[3,2048,512]{2,1,0:T(8,128)(2,1)} %win_hbm.1, bf16[512,2048]{1,0:T(8,128)(2,1)} %wout_hbm.1, bf16[2048,96]{1,0:T(8,128)(2,1)} %copy.16.d1_ref, bf16[96,512]{1,0:T(8,128)(2,1)} %d2_ref.1, ...), custom_call_target="tpu_custom_call" | custom-call | tf_op jit(solution)/shard_map/pallas_call | solution.py:316
  55.5 1.6 %copy.19 = bf16[32,2048]{1,0:T(8,128)(2,1)} copy(bf16[32,2048]{1,0:T(8,128)(2,1)} %shard_map.145) | data formatting | bytes 262144
where the time goes:
time: 57.4 us; the launch traced here: 57.1 us
  Pallas kernels  50.1 us (87%)
  local copies, waits for them, and re-layouts  6.96 us (12%)
    pallas_call x1, Pallas kernels, shards(): pl.pallas_call(functools.partial(kernel, n_seq, n_wt, hops), out_shape=ja...  50.1 us
    unnamed x3, local copies, waits for them, and re-layouts  5.58 us
    another operation x1, local copies, waits for them, and re-layouts, shards(): jnp.stack([decay_channel_bias, learning_rate_bias, prenorm_key_scale, wri...  1.39 us

commit v1 on v0

--- a/solution.py
+++ b/solution.py
@@ -56,7 +56,7 @@
 def block_terms(recept, keys, values, decay_in, rate_in, chan, seg_c, seg_r, seg_last):
     rows, width = keys.shape
     heads = width // HS
-    decay_bias, rate_bias, key_scale, share = (chan[i : i + 1] for i in range(4))
+    decay_bias, rate_bias, key_scale, share = chan[:4]
     logw = -LOG_SCALE * jax.nn.sigmoid(decay_bias + decay_in)
     rate = jax.nn.sigmoid(rate_bias + rate_in)
     row = lax.broadcasted_iota(jnp.int32, (rows, rows), 0)
@@ -117,20 +117,27 @@
     small_r = lax.broadcasted_iota(jnp.int32, (HS, HS), 0)
     small_c = lax.broadcasted_iota(jnp.int32, (HS, HS), 1)
     decay_all = jnp.exp(last) * jnp.where(seg_last == 0, 1.0, 0.0)
-    reads, offsets, maps, adds = [], [], [], []
+    maps, adds, pending = [], [], []
     for h in range(heads):
         s = head_slice(h)
         v = values[:, s].astype(BF16)
         kv = mm(jnp.concatenate([a_uk[h], a_qk[h]], axis=0), v)
-        solved = mm(inverse[h], jnp.concatenate([u_0[:, s], kv[:rows]], axis=1))
-        out = jnp.concatenate([q_0[:, s], kv[rows:]], axis=1) - mm(a_qr[h], solved)
-        reads.append(out[:, :HS])
-        offsets.append(out[:, HS:])
+        solved = mm(inverse[h], jnp.concatenate([u_0[:, s], kv[:rows]], axis=1)).astype(BF16)
         end = mm(r_e[:, s], solved, 0, 0)
         diag = jnp.where(small_r == small_c, jnp.broadcast_to(decay_all[:, s], (HS, HS)), 0.0)
         maps.append(diag - end[:, :HS])
         adds.append(mm(k_e[:, s], v, 0, 0) - end[:, HS:])
-    return reads, offsets, maps, adds, keys_mod
+        pending.append((a_qr[h], solved, q_0[:, s], kv[rows:]))
+    return maps, adds, pending, keys_mod
+
+
+def read_terms(pending):
+    reads, offsets = [], []
+    for a_qr, solved, q_0, direct in pending:
+        out = jnp.concatenate([q_0, direct], axis=1) - mm(a_qr, solved)
+        reads.append(out[:, :HS].astype(BF16))
+        offsets.append(out[:, HS:])
+    return reads, offsets
 
 
 def finish_heads(heads_y, recept, keys_mod, values, coefficient, gain):
@@ -147,10 +154,11 @@
 
 def kernel(
     n_seq, n_wt, hops,
-    x_ref, rates_ref, win_hbm, wout_hbm, d1_ref, d2_ref, a1_ref, a2_ref, chan_ref, len_ref,
+    x_ref, rates_ref, win_hbm, wout_hbm, d1_ref, d2_ref, a1_ref, a2_ref,
+    db_ref, rb_ref, ks_ref, sh_ref, co_ref, ga_ref, len_ref,
     out_ref,
-    x_all, edge_src, edge_in, win, wout, lo_src, lo_in, part, part_16, rs_in,
-    w_sem, edge_sem, fwd_sem, x_send, x_recv, lo_send, lo_recv, rs_send, rs_recv,
+    x_all, edge_src, edge_in, win, wout, lo_src, lo_in, part, part_16, rs_in, pair_in, chip_src,
+    w_sem, pair_sem, edge_sem, fwd_sem, x_send, x_recv, lo_send, lo_recv, rs_send, rs_recv,
 ):
     b = lax.axis_index("seq")
     w = lax.axis_index("wt")
@@ -158,6 +166,7 @@
     rows = shard * n_wt
     width = win.shape[2]
     heads = width // HS
+    odd = lax.rem(b, 2)
     piece = model // 8
 
     loads = [pltpu.make_async_copy(win_hbm.at[c], win.at[c], w_sem.at[c]) for c in range(3)]
@@ -233,42 +242,66 @@
         delta = previous - current
         for c in range(5):
             mixed = (current + delta * rates_ref[c : c + 1, cols]).astype(BF16)
-            weight = (
-                win[c, cols, :] if c < 3 else (d1_ref if c == 3 else a1_ref)[cols, :]
-            )
-            term = jnp.dot(mixed, weight, preferred_element_type=F32)
+            if c < 3:
+                term = mm(mixed, win[c, cols, :])
+            else:
+                term = mm(mixed, (d1_ref if c == 3 else a1_ref)[:, cols], 1, 1)
             sums[c] = term if sums[c] is None else sums[c] + term
     recept, keys, values = sums[:3]
     decay_in = jnp.dot(jnp.tanh(sums[3]).astype(BF16), d2_ref[...], preferred_element_type=F32)
     rate_in = jnp.dot(sums[4].astype(BF16), a2_ref[...], preferred_element_type=F32)
-    chan = chan_ref[...]
-    reads, offsets, maps, adds, keys_mod = block_terms(
+    chan = [ref[...] for ref in (db_ref, rb_ref, ks_ref, sh_ref, co_ref, ga_ref)]
+    maps, adds, pending, keys_mod = block_terms(
         recept, keys, values, decay_in, rate_in, chan, seg_c, seg_r, seg_last
     )
     for h in range(heads):
         lo_src[0, :, head_slice(h)] = maps[h].astype(STATE_TYPE)
         lo_src[1, :, head_slice(h)] = adds[h].astype(STATE_TYPE)
+    pair_copy = remote(lo_src, pair_in, pair_sem.at[0], pair_sem.at[1], (b + 1 - 2 * odd, w))
+    pair_copy.start()
+    reads, offsets = read_terms(pending)
+    pair_copy.wait_recv()
+    is_odd = odd == 1
+    mine_lo = lo_src[...].astype(F32)
+    other_lo = pair_in[...].astype(F32)
+    even_lo = jnp.where(is_odd, other_lo, mine_lo)
+    odd_lo = jnp.where(is_odd, mine_lo, other_lo)
+    for h in range(heads):
+        s = head_slice(h)
+        both = mm(odd_lo[0, :, s], jnp.concatenate([even_lo[0, :, s], even_lo[1, :, s]], axis=1))
+        chip_src[0, :, s] = both[:, :HS].astype(STATE_TYPE)
+        chip_src[1, :, s] = (both[:, HS:] + odd_lo[1, :, s]).astype(STATE_TYPE)
     lo_copies = [
-        remote(lo_src, lo_in.at[d - 1], lo_send.at[d - 1], lo_recv.at[d - 1], seq_peer(d))
+        remote(chip_src, lo_in.at[d - 1], lo_send.at[d - 1], lo_recv.at[d - 1], seq_peer(2 * d))
         for d in range(1, hops)
     ]
     lo_copies.append(
         remote(
-            lo_src.at[1], lo_in.at[hops - 1, 1], lo_send.at[hops - 1], lo_recv.at[hops - 1], seq_peer(hops)
+            chip_src.at[1], lo_in.at[hops - 1, 1], lo_send.at[hops - 1], lo_recv.at[hops - 1],
+            seq_peer(2 * hops),
         )
     )
     for copy in lo_copies:
         copy.start()
     for copy in lo_copies:
         copy.wait_recv()
+    lo_copies.append(pair_copy)
     state = [lo_in[hops - 1, 1, :, head_slice(h)].astype(F32) for h in range(heads)]
     for d in range(hops - 2, -1, -1):
         state = [
             mm(lo_in[d, 0, :, head_slice(h)], state[h]) + lo_in[d, 1, :, head_slice(h)].astype(F32)
             for h in range(heads)
         ]
+    state = [
+        jnp.where(
+            is_odd,
+            mm(even_lo[0, :, head_slice(h)], state[h]) + even_lo[1, :, head_slice(h)],
+            state[h],
+        )
+        for h in range(heads)
+    ]
     heads_y = [mm(reads[h], state[h]) + offsets[h] for h in range(heads)]
-    head_mix = finish_heads(heads_y, recept, keys_mod, values, chan[4:5], chan[5:6])
+    head_mix = finish_heads(heads_y, recept, keys_mod, values, chan[4], chan[5])
 
     loads[3].wait()
     for k in range(0, model, step):
@@ -303,20 +336,21 @@
     shard, model = layer_input.shape
     rows = shard * n_wt
     width = decay_lowrank_second.shape[1]
-    hops = (n_seq + 1) // 2
-    chan = jnp.stack(
-        [
+    hops = (n_seq // 2 + 1) // 2
+    chan = [
+        v.reshape(1, width)
+        for v in (
             decay_channel_bias, learning_rate_bias, prenorm_key_scale,
             written_key_share, present_step_coefficient, head_norm_gain,
-        ]
-    )
+        )
+    ]
     vmem = pl.BlockSpec(memory_space=pltpu.VMEM)
     far = pl.BlockSpec(memory_space=pl.ANY)
     dma = pltpu.SemaphoreType.DMA
     return pl.pallas_call(
         functools.partial(kernel, n_seq, n_wt, hops),
         out_shape=jax.ShapeDtypeStruct((shard, model), BF16),
-        in_specs=[vmem, vmem, far, far, vmem, vmem, vmem, vmem, vmem, pl.BlockSpec(memory_space=pltpu.SMEM)],
+        in_specs=[vmem, vmem, far, far] + [vmem] * 10 + [pl.BlockSpec(memory_space=pltpu.SMEM)],
         out_specs=vmem,
         scratch_shapes=[
             pltpu.VMEM((rows, model), BF16),
@@ -329,7 +363,9 @@
             pltpu.VMEM((rows, model), F32),
             pltpu.VMEM((rows, model), BF16),
             pltpu.VMEM((n_wt - 1, shard, model), BF16),
-            dma((4,)), dma((2,)), dma((n_wt - 1,)),
+            pltpu.VMEM((2, HS, width), STATE_TYPE),
+            pltpu.VMEM((2, HS, width), STATE_TYPE),
+            dma((4,)), dma((2,)), dma((2,)), dma((n_wt - 1,)),
             dma((n_wt - 1,)), dma((n_wt - 1,)),
             dma((hops,)), dma((hops,)),
             dma((n_wt - 1,)), dma((n_wt - 1,)),
@@ -339,8 +375,8 @@
         ),
     )(
         layer_input, token_shift_rates, input_projection_weight, output_matrix,
-        decay_lowrank_first, decay_lowrank_second, learning_rate_first, learning_rate_second,
-        chan, packed_request_length,
+        decay_lowrank_first.T, decay_lowrank_second, learning_rate_first.T, learning_rate_second,
+        *chan, packed_request_length,
     )
 
 

time: 57.4 us -> 49.4 us (0.86)
  local copies, waits for them, and re-layouts: 6.96 us -> 1.57 us
  Pallas kernels: 50.1 us -> 47.7 us
    unnamed x3 -> x1, local copies, waits for them, and re-layouts: 5.58 us -> 1.57 us
    pallas_call x1, Pallas kernels: 50.1 us -> 47.7 us  [shards(): pl.pallas_call(functools.partial(kernel, n_seq, n_wt, hops), out_shape=ja...]
    another operation x1 -> x0, local copies, waits for them, and re-layouts: 1.39 us -> none  [shards(): jnp.stack([decay_channel_bias, learning_rate_bias, prenorm_key_scale, wri...]
where the time goes in v1:
time: 49.4 us; the launch traced here: 49.3 us
  Pallas kernels  47.7 us (97%)
  local copies, waits for them, and re-layouts  1.57 us (3%)
    pallas_call x1, Pallas kernels, shards(): pl.pallas_call(functools.partial(kernel, n_seq, n_wt, hops), out_shape=ja...  47.7 us
    unnamed x1, local copies, waits for them, and re-layouts  1.57 us

profile of v1, /device:TPU:24, one launch (start us, length us, event | category | flops | bytes accessed | tf_op | source)
XLA Modules:
  0.0 49.3 jit_solution(15822777362783015113)
XLA Ops:
  0.0 47.7 %shard_map.145 = bf16[32,2048]{1,0:T(8,128)(2,1)} custom-call(bf16[32,2048]{1,0:T(8,128)(2,1)} %x_ref.1, f32[5,2048]{1,0:T(8,128)} %rates_ref.1, bf16[3,2048,512]{2,1,0:T(8,128)(2,1)} %win_hbm.1, bf16[512,2048]{1,0:T(8,128)(2,1)} %wout_hbm.1, bf16[96,2048]{1,0:T(8,128)(2,1)} %bitcast.8, bf16[96,512]{1,0:T(8,128)(2,1)} %d2_ref.1, bf16[96,2048]{1,0:T(8,128)(2,1)} %bitcast.9, ...), custom_call_target="tpu_custom_call" | custom-call | tf_op jit(solution)/shard_map/pallas_call | solution.py:350
  47.7 1.6 %copy.17 = bf16[32,2048]{1,0:T(8,128)(2,1)} copy(bf16[32,2048]{1,0:T(8,128)(2,1)} %shard_map.145) | data formatting | bytes 262144

commit v2 on v1

--- a/solution.py
+++ b/solution.py
@@ -157,7 +157,7 @@
     x_ref, rates_ref, win_hbm, wout_hbm, d1_ref, d2_ref, a1_ref, a2_ref,
     db_ref, rb_ref, ks_ref, sh_ref, co_ref, ga_ref, len_ref,
     out_ref,
-    x_all, edge_src, edge_in, win, wout, lo_src, lo_in, part, part_16, rs_in, pair_in, chip_src,
+    x_all, edge_src, edge_in, win, wout, lo_src, lo_in, part, acc, rs_src, rs_in, pair_in, chip_src,
     w_sem, pair_sem, edge_sem, fwd_sem, x_send, x_recv, lo_send, lo_recv, rs_send, rs_recv,
 ):
     b = lax.axis_index("seq")
@@ -207,12 +207,37 @@
     def _():
         edge_copy.start()
 
-    x_copies = [
-        remote(x_ref, x_all.at[mine], x_send.at[d - 1], x_recv.at[d - 1], wt_peer(d))
-        for d in range(1, n_wt)
-    ]
-    for copy in x_copies:
-        copy.start()
+    half = shard // 2
+
+    def line_copy(step, part_no, up):
+        owner = w - step if up else w + step
+        place = x_all.at[pl.ds(pl.multiple_of(owner * shard + part_no * half, half), half)]
+        side = 0 if up else 1
+        return remote(
+            place, place, x_send.at[side, step, part_no], x_recv.at[side, step, part_no],
+            (b, w + 1 if up else w - 1),
+        )
+
+    def sends(step, up):
+        return jnp.logical_and(w >= step, w + 1 < n_wt) if up else jnp.logical_and(w + step < n_wt, w >= 1)
+
+    def gets(step, up):
+        return w - 1 - step >= 0 if up else w + 1 + step < n_wt
+
+    def line_step(step, part_no, up):
+        if step > 0:
+            @pl.when(gets(step - 1, up))
+            def _():
+                line_copy(step - 1, part_no, up).wait_recv()
+
+        if step < n_wt - 1:
+            @pl.when(sends(step, up))
+            def _():
+                line_copy(step, part_no, up).start()
+
+    for part_no in range(2):
+        for up in (True, False):
+            line_step(0, part_no, up)
     edge_copy.wait_recv()
 
     @pl.when(is_last)
@@ -223,8 +248,10 @@
         for copy in forwards:
             copy.wait_send()
 
-    for copy in x_copies:
-        copy.wait_recv()
+    for step in range(1, n_wt):
+        for part_no in range(2):
+            for up in (True, False):
+                line_step(step, part_no, up)
     for load in loads[:3]:
         load.wait()
 
@@ -308,22 +335,74 @@
         cols = slice(k, k + step)
         term = jnp.dot(head_mix, wout[:, cols], preferred_element_type=F32)
         part[:, cols] = term
-        part_16[:, cols] = term.astype(BF16)
-    rs_copies = []
-    for d in range(1, n_wt):
-        there = pl.ds(pl.multiple_of(lax.rem(w + d, n_wt) * shard, shard), shard)
-        rs_copies.append(
-            remote(part_16.at[there], rs_in.at[d - 1], rs_send.at[d - 1], rs_recv.at[d - 1], wt_peer(d))
-        )
-    for copy in rs_copies:
-        copy.start()
-    total = part[mine, :] + x_ref[...].astype(F32)
-    for d, copy in enumerate(rs_copies):
-        copy.wait_recv()
-        total = total + rs_in[d].astype(F32)
-    out_ref[...] = total.astype(out_ref.dtype)
-    for copy in x_copies + lo_copies + rs_copies:
+    def owner_rows(owner, part_no):
+        return pl.ds(pl.multiple_of(owner * shard + part_no * half, half), half)
+
+    def sum_copy(step, part_no, up):
+        owner = n_wt - 1 - step if up else step
+        side = 0 if up else 1
+        return remote(
+            rs_src.at[side, step, part_no], rs_in.at[side, step, part_no],
+            rs_send.at[side, step, part_no], rs_recv.at[side, step, part_no],
+            (b, w + 1 if up else w - 1),
+        ), owner
+
+    def on_way(owner, up):
+        return w < owner if up else w > owner
+
+    for step in range(n_wt - 1):
+        for part_no in range(2):
+            for up in (True, False):
+                copy, owner = sum_copy(step, part_no, up)
+                side = 0 if up else 1
+                inner = (w > 0) if up else (w < n_wt - 1)
+                own = slice(owner * shard + part_no * half, owner * shard + (part_no + 1) * half)
+
+                @pl.when(on_way(owner, up))
+                def _():
+                    @pl.when(inner)
+                    def _():
+                        copy.wait_recv()
+                        rs_src[side, step, part_no] = (
+                            part[own, :] + rs_in[side, step, part_no].astype(F32)
+                        ).astype(BF16)
+
+                    @pl.when(jnp.logical_not(inner))
+                    def _():
+                        rs_src[side, step, part_no] = part[own, :].astype(BF16)
+
+                    copy.start()
+
+    for part_no in range(2):
+        here = slice(part_no * half, (part_no + 1) * half)
+        out_ref_rows = owner_rows(w, part_no)
+        acc[here, :] = part[out_ref_rows, :] + x_ref[here, :].astype(F32)
+        for step in range(n_wt):
+            for up in (True, False):
+                if step < n_wt - 1:
+                    copy, owner = sum_copy(step, part_no, up)
+                    side = 0 if up else 1
+                    inner = (w > 0) if up else (w < n_wt - 1)
+
+                    @pl.when(jnp.logical_and(w == owner, inner))
+                    def _():
+                        copy.wait_recv()
+                        acc[here, :] += rs_in[side, step, part_no].astype(F32)
+    out_ref[...] = acc[...].astype(out_ref.dtype)
+    for copy in lo_copies:
         copy.wait_send()
+    for step in range(n_wt - 1):
+        for part_no in range(2):
+            for up in (True, False):
+                copy, owner = sum_copy(step, part_no, up)
+
+                @pl.when(sends(step, up))
+                def _():
+                    line_copy(step, part_no, up).wait_send()
+
+                @pl.when(on_way(owner, up))
+                def _():
+                    copy.wait_send()
 
 
 def shards(
@@ -361,14 +440,15 @@
             pltpu.VMEM((2, HS, width), STATE_TYPE),
             pltpu.VMEM((hops, 2, HS, width), STATE_TYPE),
             pltpu.VMEM((rows, model), F32),
-            pltpu.VMEM((rows, model), BF16),
-            pltpu.VMEM((n_wt - 1, shard, model), BF16),
+            pltpu.VMEM((shard, model), F32),
+            pltpu.VMEM((2, n_wt - 1, 2, shard // 2, model), BF16),
+            pltpu.VMEM((2, n_wt - 1, 2, shard // 2, model), BF16),
             pltpu.VMEM((2, HS, width), STATE_TYPE),
             pltpu.VMEM((2, HS, width), STATE_TYPE),
             dma((4,)), dma((2,)), dma((2,)), dma((n_wt - 1,)),
-            dma((n_wt - 1,)), dma((n_wt - 1,)),
+            dma((2, n_wt - 1, 2)), dma((2, n_wt - 1, 2)),
             dma((hops,)), dma((hops,)),
-            dma((n_wt - 1,)), dma((n_wt - 1,)),
+            dma((2, n_wt - 1, 2)), dma((2, n_wt - 1, 2)),
         ],
         compiler_params=pltpu.CompilerParams(
             collective_id=0, has_side_effects=True, vmem_limit_bytes=56 * 1024 * 1024

time: 49.4 us -> 59 us (1.19)
  the two profiles are of different devices: /device:TPU:24 before, /device:TPU:0 now
where the time goes in v2:
time: 59 us; the launch traced here: 58.9 us
  Pallas kernels  57.3 us (97%)
  local copies, waits for them, and re-layouts  1.57 us (3%)
    pallas_call x1, Pallas kernels, shards(): pl.pallas_call(functools.partial(kernel, n_seq, n_wt, hops), out_shape=ja...  57.3 us
    unnamed x1, local copies, waits for them, and re-layouts  1.57 us

profile of v2, /device:TPU:0, one launch (start us, length us, event | category | flops | bytes accessed | tf_op | source)
XLA Modules:
  0.0 58.9 jit_solution(3958999220222882173)
XLA Ops:
  0.0 57.3 %shard_map.145 = bf16[32,2048]{1,0:T(8,128)(2,1)} custom-call(bf16[32,2048]{1,0:T(8,128)(2,1)} %x_ref.1, f32[5,2048]{1,0:T(8,128)} %rates_ref.1, bf16[3,2048,512]{2,1,0:T(8,128)(2,1)} %win_hbm.1, bf16[512,2048]{1,0:T(8,128)(2,1)} %wout_hbm.1, bf16[96,2048]{1,0:T(8,128)(2,1)} %bitcast.8, bf16[96,512]{1,0:T(8,128)(2,1)} %d2_ref.1, bf16[96,2048]{1,0:T(8,128)(2,1)} %bitcast.9, ...), custom_call_target="tpu_custom_call" | custom-call | tf_op jit(solution)/shard_map/pallas_call | solution.py:429
  57.3 1.6 %copy.17 = bf16[32,2048]{1,0:T(8,128)(2,1)} copy(bf16[32,2048]{1,0:T(8,128)(2,1)} %shard_map.145) | data formatting | bytes 262144

commit v3 on v1

--- a/solution.py
+++ b/solution.py
@@ -211,20 +211,45 @@
         remote(x_ref, x_all.at[mine], x_send.at[d - 1], x_recv.at[d - 1], wt_peer(d))
         for d in range(1, n_wt)
     ]
-    for copy in x_copies:
-        copy.start()
-    edge_copy.wait_recv()
+    top = n_wt - 1
+    relayed = [d for d in (2, n_wt - 2)] if n_wt > 3 else []
+    order = sorted(range(1, n_wt), key=lambda d: (d not in relayed, d))
+
+    def direct(d):
+        if not relayed or d not in (1, top):
+            return w >= 0
+        return w != (top if d == 1 else 0)
+
+    def relay_copy(owner, target, d):
+        place = x_all.at[pl.ds(owner * shard, shard)]
+        return remote(place, place, fwd_sem.at[n_wt - 1], x_recv.at[d - 1], (b, target))
+
+    relays = [(n_wt - 2, 0, top, top), (1, top, 0, 1)] if relayed else []
+    for d in order:
+        @pl.when(direct(d))
+        def _():
+            x_copies[d - 1].start()
 
     @pl.when(is_last)
     def _():
+        edge_copy.wait_recv()
         for copy in forwards:
             copy.start()
-        edge_copy.wait_send()
-        for copy in forwards:
-            copy.wait_send()
-
-    for copy in x_copies:
-        copy.wait_recv()
+
+    for d in sorted(set(relayed)):
+        x_copies[d - 1].wait_recv()
+    for at, owner, target, d in relays:
+        @pl.when(w == at)
+        def _():
+            relay_copy(owner, target, d).start()
+
+    @pl.when(w != top)
+    def _():
+        edge_copy.wait_recv()
+
+    for d in range(1, n_wt):
+        if d not in relayed:
+            x_copies[d - 1].wait_recv()
     for load in loads[:3]:
         load.wait()
 
@@ -322,8 +347,23 @@
         copy.wait_recv()
         total = total + rs_in[d].astype(F32)
     out_ref[...] = total.astype(out_ref.dtype)
-    for copy in x_copies + lo_copies + rs_copies:
+    for copy in lo_copies + rs_copies:
         copy.wait_send()
+    for d in range(1, n_wt):
+        @pl.when(direct(d))
+        def _():
+            x_copies[d - 1].wait_send()
+
+    for at, owner, target, d in relays:
+        @pl.when(w == at)
+        def _():
+            relay_copy(owner, target, d).wait_send()
+
+    @pl.when(is_last)
+    def _():
+        edge_copy.wait_send()
+        for copy in forwards:
+            copy.wait_send()
 
 
 def shards(
@@ -365,7 +405,7 @@
             pltpu.VMEM((n_wt - 1, shard, model), BF16),
             pltpu.VMEM((2, HS, width), STATE_TYPE),
             pltpu.VMEM((2, HS, width), STATE_TYPE),
-            dma((4,)), dma((2,)), dma((2,)), dma((n_wt - 1,)),
+            dma((4,)), dma((2,)), dma((2,)), dma((n_wt,)),
             dma((n_wt - 1,)), dma((n_wt - 1,)),
             dma((hops,)), dma((hops,)),
             dma((n_wt - 1,)), dma((n_wt - 1,)),

time: 49.4 us -> 46.6 us (0.943)
  Pallas kernels: 47.7 us -> 44.9 us
    pallas_call x1, Pallas kernels: 47.7 us -> 44.9 us  [shards(): pl.pallas_call(functools.partial(kernel, n_seq, n_wt, hops), out_shape=ja...]
where the time goes in v3:
time: 46.6 us; the launch traced here: 46.5 us
  Pallas kernels  44.9 us (96%)
  local copies, waits for them, and re-layouts  1.57 us (3%)
    pallas_call x1, Pallas kernels, shards(): pl.pallas_call(functools.partial(kernel, n_seq, n_wt, hops), out_shape=ja...  44.9 us
    unnamed x1, local copies, waits for them, and re-layouts  1.57 us

profile of v3, /device:TPU:24, one launch (start us, length us, event | category | flops | bytes accessed | tf_op | source)
XLA Modules:
  0.0 46.5 jit_solution(13996422391662277892)
XLA Ops:
  0.0 44.9 %shard_map.145 = bf16[32,2048]{1,0:T(8,128)(2,1)} custom-call(bf16[32,2048]{1,0:T(8,128)(2,1)} %x_ref.1, f32[5,2048]{1,0:T(8,128)} %rates_ref.1, bf16[3,2048,512]{2,1,0:T(8,128)(2,1)} %win_hbm.1, bf16[512,2048]{1,0:T(8,128)(2,1)} %wout_hbm.1, bf16[96,2048]{1,0:T(8,128)(2,1)} %bitcast.8, bf16[96,512]{1,0:T(8,128)(2,1)} %d2_ref.1, bf16[96,2048]{1,0:T(8,128)(2,1)} %bitcast.9, ...), custom_call_target="tpu_custom_call" | custom-call | tf_op jit(solution)/shard_map/pallas_call | solution.py:390
  44.9 1.6 %copy.17 = bf16[32,2048]{1,0:T(8,128)(2,1)} copy(bf16[32,2048]{1,0:T(8,128)(2,1)} %shard_map.145) | data formatting | bytes 262144

commit v4 on v3

--- a/solution.py
+++ b/solution.py
@@ -157,8 +157,8 @@
     x_ref, rates_ref, win_hbm, wout_hbm, d1_ref, d2_ref, a1_ref, a2_ref,
     db_ref, rb_ref, ks_ref, sh_ref, co_ref, ga_ref, len_ref,
     out_ref,
-    x_all, edge_src, edge_in, win, wout, lo_src, lo_in, part, part_16, rs_in, pair_in, chip_src,
-    w_sem, pair_sem, edge_sem, fwd_sem, x_send, x_recv, lo_send, lo_recv, rs_send, rs_recv,
+    x_all, edge_src, edge_in, win, wout, lo_src, lo_in, part, part_16, rs_in, pair_in, chip_src, merge_in, acc,
+    w_sem, merge_sem, pair_sem, edge_sem, fwd_sem, x_send, x_recv, lo_send, lo_recv, rs_send, rs_recv,
 ):
     b = lax.axis_index("seq")
     w = lax.axis_index("wt")
@@ -340,19 +340,63 @@
         rs_copies.append(
             remote(part_16.at[there], rs_in.at[d - 1], rs_send.at[d - 1], rs_recv.at[d - 1], wt_peer(d))
         )
-    for copy in rs_copies:
-        copy.start()
-    total = part[mine, :] + x_ref[...].astype(F32)
-    for d, copy in enumerate(rs_copies):
-        copy.wait_recv()
-        total = total + rs_in[d].astype(F32)
+    def end_rows(owner):
+        return slice(owner * shard, (owner + 1) * shard)
+
+    merges = [(0, 1, top, n_wt - 2), (top, top - 1, 0, 2)] if relayed else []
+
+    def merge_copy(owner, target):
+        return remote(part_16.at[pl.ds(owner * shard, shard)], merge_in, merge_sem.at[0], merge_sem.at[1], (b, target))
+
+    def at_once(d):
+        held = [jnp.logical_and(w == at, d == which) for _, at, _, which in merges if d == which]
+        fine = direct(d)
+        for one in held:
+            fine = jnp.logical_and(fine, jnp.logical_not(one))
+        return fine
+
+    for end, at, owner, which in merges:
+        @pl.when(w == end)
+        def _():
+            merge_copy(owner, at).start()
+
+    for d in order:
+        @pl.when(at_once(d))
+        def _():
+            rs_copies[d - 1].start()
+
+    for end, at, owner, which in merges:
+        @pl.when(w == at)
+        def _():
+            merge_copy(owner, at).wait_recv()
+            part_16[end_rows(owner), :] = (
+                part[end_rows(owner), :] + merge_in[...].astype(F32)
+            ).astype(BF16)
+            rs_copies[which - 1].start()
+
+    acc[...] = part[mine, :] + x_ref[...].astype(F32)
+    for d in sorted(range(1, n_wt), key=lambda d: (d in relayed, d)):
+        absent = w == (0 if d == 1 else top) if relayed and d in (1, top) else w < 0
+
+        @pl.when(jnp.logical_not(absent))
+        def _():
+            rs_copies[d - 1].wait_recv()
+            acc[...] += rs_in[d - 1].astype(F32)
+
+    total = acc[...]
     out_ref[...] = total.astype(out_ref.dtype)
-    for copy in lo_copies + rs_copies:
+    for copy in lo_copies:
         copy.wait_send()
     for d in range(1, n_wt):
         @pl.when(direct(d))
         def _():
             x_copies[d - 1].wait_send()
+            rs_copies[d - 1].wait_send()
+
+    for end, at, owner, which in merges:
+        @pl.when(w == end)
+        def _():
+            merge_copy(owner, at).wait_send()
 
     for at, owner, target, d in relays:
         @pl.when(w == at)
@@ -405,7 +449,9 @@
             pltpu.VMEM((n_wt - 1, shard, model), BF16),
             pltpu.VMEM((2, HS, width), STATE_TYPE),
             pltpu.VMEM((2, HS, width), STATE_TYPE),
-            dma((4,)), dma((2,)), dma((2,)), dma((n_wt,)),
+            pltpu.VMEM((shard, model), BF16),
+            pltpu.VMEM((shard, model), F32),
+            dma((4,)), dma((2,)), dma((2,)), dma((2,)), dma((n_wt,)),
             dma((n_wt - 1,)), dma((n_wt - 1,)),
             dma((hops,)), dma((hops,)),
             dma((n_wt - 1,)), dma((n_wt - 1,)),

time: 46.6 us -> 46.6 us (level)
  the two profiles are of different devices: /device:TPU:24 before, /device:TPU:0 now
where the time goes in v4:
time: 46.6 us; the launch traced here: 46.5 us
  Pallas kernels  44.9 us (96%)
  local copies, waits for them, and re-layouts  1.57 us (3%)
    pallas_call x1, Pallas kernels, shards(): pl.pallas_call(functools.partial(kernel, n_seq, n_wt, hops), out_shape=ja...  44.9 us
    unnamed x1, local copies, waits for them, and re-layouts  1.57 us

profile of v4, /device:TPU:0, one launch (start us, length us, event | category | flops | bytes accessed | tf_op | source)
XLA Modules:
  0.0 46.5 jit_solution(6514999365048714711)
XLA Ops:
  0.0 44.9 %shard_map.145 = bf16[32,2048]{1,0:T(8,128)(2,1)} custom-call(bf16[32,2048]{1,0:T(8,128)(2,1)} %x_ref.1, f32[5,2048]{1,0:T(8,128)} %rates_ref.1, bf16[3,2048,512]{2,1,0:T(8,128)(2,1)} %win_hbm.1, bf16[512,2048]{1,0:T(8,128)(2,1)} %wout_hbm.1, bf16[96,2048]{1,0:T(8,128)(2,1)} %bitcast.8, bf16[96,512]{1,0:T(8,128)(2,1)} %d2_ref.1, bf16[96,2048]{1,0:T(8,128)(2,1)} %bitcast.9, ...), custom_call_target="tpu_custom_call" | custom-call | tf_op jit(solution)/shard_map/pallas_call | solution.py:434
  44.9 1.6 %copy.17 = bf16[32,2048]{1,0:T(8,128)(2,1)} copy(bf16[32,2048]{1,0:T(8,128)(2,1)} %shard_map.145) | data formatting | bytes 262144
